TPU v7x, 32 devices: a whole 2x2x4 slice. The times are simulated.
32 devices in a mesh: leaf: 16 (over z, y, x), col: 2 (over core).
Axes of the slice: x: 2, y: 2, z: 4, core: 2. Of those that a mesh axis runs over, the one named last changes fastest.
Arguments:
- sources: bfloat16 [65536, 256], P('leaf', 'col'), may hold values from -6 to 6
- near_tiles: bfloat16 [256, 8, 256, 256], P('leaf', 'col'), may hold values from -0.125 to 0.125
- near_index: int32 [256, 8], P('leaf'), may hold values from 0 to 255, as said below
- near_count: int32 [256], P('leaf'), may hold values from 1 to 8, as said below
- leaf_basis: bfloat16 [256, 64, 256], P('leaf'), may hold values from -0.375 to 0.375
- leaf_coupling: bfloat16 [256, 64, 256], P('leaf'), may hold values from -0.375 to 0.375
- leaf_far: int32 [256, 4], P('leaf'), may hold values from 0 to 255, as said below
- up_leaf: bfloat16 [32, 64, 512], P('leaf'), may hold values from -0.25 to 0.25
- mid_coupling: bfloat16 [32, 64, 256], P('leaf'), may hold values from -0.375 to 0.375
- mid_far: int32 [32, 4], P('leaf'), may hold values from 0 to 31, as said below
- up_mid: bfloat16 [32, 64, 64], P('leaf'), may hold values from -0.75 to 0.75
- top_coupling: bfloat16 [4, 64, 256], replicated, may hold values from -0.4375 to 0.4375
Outputs:
- product: float32 [65536, 256], P('leaf', 'col')
Inputs may be any that keep to these rules, and one draw needn't show every extreme that they name: `near_index`: entry 0 of row i is i; the other 7 entries are distinct leaves j with j != i and |i - j| <= 8. Only the first near_count[i] slots of leaf i count; some leaf has all 8. `leaf_far`: row i holds 4 distinct leaves j != i with |i // 8 - j // 8| <= 1. `mid_far`: row a holds 4 distinct middle clusters b != a with |a // 8 - b // 8| <= 1.
All inputs are finite; a program needn't handle non-finite values.
Results may differ from a plain program's by a relative error of at most 0.01.
Values may be sent and summed in bfloat16 or wider, within the bound.
No kernel may reach another device: no remote copies, remote signals or barrier semaphores. Data moves between devices by JAX's collectives and lax.ppermute only.
A program may use at most 128 MiB of HBM per device.

v0:
```python
import jax
import jax.numpy as jnp
from jax import lax
from jax.sharding import PartitionSpec as P

CHILD = 8
FAR = 4


def padded(x, sides, width):
    for axis, dim in sides:
        size, length = (lax.axis_size(axis), x.shape[dim])
        up = [(i, (i + 1) % size) for i in range(size - 1)]
        down = [(j, i) for i, j in up]
        last = lax.slice_in_dim(x, length - width, length, axis=dim)
        first = lax.slice_in_dim(x, 0, width, axis=dim)
        before = lax.ppermute(last, axis, up)
        after = lax.ppermute(first, axis, down)
        x = jnp.concatenate([before, x, after], axis=dim)
    return x


def shards(
    sources,
    near_tiles,
    near_index,
    near_count,
    leaf_basis,
    leaf_coupling,
    leaf_far,
    up_leaf,
    mid_coupling,
    mid_far,
    up_mid,
    top_coupling,
):
    f32 = jnp.float32
    bf16 = jnp.bfloat16
    leaf_count = leaf_basis.shape[0]
    rank_size = leaf_basis.shape[1]
    leaf_size = leaf_basis.shape[2]
    col_count = sources.shape[1]
    mid_count = leaf_count // CHILD
    total_top = top_coupling.shape[0]
    device = lax.axis_index("leaf")
    first_leaf = device * leaf_count
    first_mid = device * mid_count
    window = padded(sources, (("leaf", 0),), CHILD * leaf_size)
    near_local = near_index - (first_leaf - CHILD)
    all_tiles = lax.all_gather(near_tiles, "col", axis=1, tiled=True)
    slot_count = all_tiles.shape[1]
    blocks = window.reshape(-1, leaf_size, window.shape[1])
    picked = blocks[near_local]
    live_mask = jnp.arange(slot_count)[None, :] < near_count[:, None]
    picked = jnp.where(live_mask[:, :, None, None], picked, jnp.zeros((), bf16))
    result = jnp.einsum("lsij,lsjc->lic", all_tiles, picked, preferred_element_type=f32)
    near_part = result.reshape(leaf_count * leaf_size, window.shape[1])
    leaf_blocks = sources.reshape(leaf_count, leaf_size, col_count)
    leaf_coef = jnp.einsum(
        "lrk,lkc->lrc", leaf_basis, leaf_blocks, preferred_element_type=f32
    ).astype(bf16)
    mid_coef = jnp.einsum(
        "qrk,qkc->qrc",
        up_leaf,
        leaf_coef.reshape(mid_count, CHILD * rank_size, col_count),
        preferred_element_type=f32,
    ).astype(bf16)
    mid_lift = jnp.einsum("qrs,qsc->qrc", up_mid, mid_coef, preferred_element_type=f32).astype(bf16)
    parent = (first_mid + jnp.arange(mid_count)) // CHILD
    mid_flat = mid_far.reshape(-1)
    top_range = jnp.arange(total_top)
    coef_piece = lax.all_gather(mid_coef, "leaf", axis=0, tiled=True)
    lift_piece = lax.all_gather(mid_lift, "leaf", axis=0, tiled=True)
    global_ids = jnp.arange(coef_piece.shape[0])
    group_map = (top_range[:, None] == (global_ids // CHILD)[None, :]).astype(bf16)
    top_total = jnp.einsum("pk,krc->prc", group_map, lift_piece, preferred_element_type=f32)
    global_ids = jnp.arange(coef_piece.shape[0])
    pick_map = (mid_flat[:, None] == global_ids[None, :]).astype(bf16)
    mid_picked = jnp.einsum("ik,krc->irc", pick_map, coef_piece, preferred_element_type=f32)
    top_coef = top_total.astype(bf16)
    parent_rows = top_coupling[parent]
    keep_mask = top_range[None, :] != parent[:, None]
    stacked = jnp.where(keep_mask[:, :, None, None], top_coef[None], jnp.zeros((), bf16))
    top_field = jnp.einsum(
        "qrk,qkc->qrc",
        parent_rows,
        stacked.reshape(mid_count, total_top * rank_size, col_count),
        preferred_element_type=f32,
    ).astype(bf16)
    mid_chosen = mid_picked.astype(bf16).reshape(mid_count, FAR * rank_size, col_count)
    mid_field = (
        jnp.einsum("qrk,qkc->qrc", mid_coupling, mid_chosen, preferred_element_type=f32)
        + jnp.einsum("qrs,qrc->qsc", up_mid, top_field, preferred_element_type=f32)
    ).astype(bf16)
    leaf_window = padded(leaf_coef, (("leaf", 0),), CHILD)
    far_local = leaf_far - (first_leaf - CHILD)
    leaf_chosen = leaf_window[far_local].reshape(leaf_count, FAR * rank_size, col_count)
    down_part = jnp.einsum("qrs,qrc->qsc", up_leaf, mid_field, preferred_element_type=f32).reshape(
        leaf_count, rank_size, col_count
    )
    leaf_field = (
        jnp.einsum("lrk,lkc->lrc", leaf_coupling, leaf_chosen, preferred_element_type=f32)
        + down_part
    ).astype(bf16)
    far_part = jnp.einsum(
        "lrk,lrc->lkc", leaf_basis, leaf_field, preferred_element_type=f32
    ).reshape(leaf_count * leaf_size, col_count)
    return near_part + far_part


def solution(mesh):
    return jax.shard_map(
        shards,
        mesh=mesh,
        in_specs=(
            P("leaf", "col"),
            P("leaf", "col", None, None),
            P("leaf", None),
            P("leaf"),
            P("leaf", None, None),
            P("leaf", None, None),
            P("leaf", None),
            P("leaf", None, None),
            P("leaf", None, None),
            P("leaf", None),
            P("leaf", None, None),
            P(),
        ),
        out_specs=P("leaf", "col"),
        check_vma=False,
    )
```

profile of v0, /device:TPU:0, one launch (start us, length us, event | category | flops | bytes accessed | tf_op | source)
XLA Modules:
  0.0 168.7 jit_solution(13844385451105794318)
XLA Ops:
  6.5 0.7 all-gather.2.cloned.1.call-update
  7.3 0.2 copy-done
  7.6 0.3 copy-done.1
  7.9 0.3 convolution_convert_fusion
  8.3 4.9 %collective-permute-start.2 = (bf16[8,64,128]{2,1,0:T(8,128)(2,1)S(1)}, bf16[8,64,128]{2,1,0:T(8,128)(2,1)S(1)}, u32[]{:S(2)}, u32[]{:S(2)}) collective-permute-start(bf16[8,64,128]{2,1,0:T(8,128)(2,1)S(1)} %get-tuple-element.7), channel_id=1, source_target_pairs={{0,2},{2,4},{4,6},{6,8},{8,10},{10,12},{12,14},{14,16},{16,18},{18... | collective-permute-start | bytes 393224 | tf_op jit(solution)/shard_map/ppermute | solution.py:17
  13.2 1.3 collective-permute-start.3
  14.5 1.1 fusion.33
  15.5 5.4 %collective-permute-start = (bf16[2048,128]{1,0:T(8,128)(2,1)}, bf16[2048,128]{1,0:T(8,128)(2,1)}, u32[]{:S(2)}, u32[]{:S(2)}) collective-permute-start(bf16[2048,128]{1,0:T(8,128)(2,1)} %get-tuple-element.5), channel_id=1, source_target_pairs={{0,2},{2,4},{4,6},{6,8},{8,10},{10,12},{12,14},{14,16},{16,18},{18... | collective-permute-start | bytes 1572872 | tf_op jit(solution)/shard_map/ppermute | solution.py:17
  20.9 1.3 collective-permute-start.1
  22.2 0.1 copy.27
  22.3 0.1 reshape.160
  22.4 0.2 convolution_convert_fusion.5
  22.6 0.1 fusion.12
  22.7 57.8 %all_gather.11 = bf16[32,64,128]{2,1,0:T(8,128)(2,1)S(1)} all-gather(bf16[2,64,128]{2,1,0:T(8,128)(2,1)S(1)} %fusion.12), channel_id=1, replica_groups=mesh['leaf'=16,'col'=2] {'leaf'}, dimensions={0}, use_global_device_ids=true | all-gather | bytes 557056 | tf_op jit(solution)/shard_map/all_gather | solution.py:73
  80.5 0.4 convolution_convert_fusion.2
  81.1 0.1 broadcast_in_dim.60
  81.2 0.1 eq.28
  81.3 38.7 %all_gather.10 = bf16[32,64,128]{2,1,0:T(8,128)(2,1)S(1)} all-gather(bf16[2,64,128]{2,1,0:T(8,128)(2,1)S(1)} %bitcast.59), channel_id=1, replica_groups=mesh['leaf'=16,'col'=2] {'leaf'}, dimensions={0}, use_global_device_ids=true | all-gather | bytes 557056 | tf_op jit(solution)/shard_map/all_gather | solution.py:72
  119.9 0.4 convolution_convert_fusion.1
  120.4 0.6 gather_fusion.2
  121.1 0.4 fusion.11
  121.5 0.4 convolution_bitcast_fusion.1
  122.0 0.1 reshape.152
  122.1 0.2 copy.33
  122.3 1.0 pad_maximum_fusion.1
  123.3 0.7 gather_fusion.1
  124.0 1.9 %fusion.9 = f32[16,128,256]{2,1,0:T(8,128)} fusion(bf16[16,64,256]{2,1,0:T(8,128)(2,1)S(1)} %copy-done, f32[16,64,128]{2,1,0:T(8,128)S(1)} %bitcast.57, bf16[16,64,256]{2,1,0:T(8,128)(2,1)S(1)} %copy-done.3, bf16[16,256,128]{2,1,0:T(8,128)(2,1)S(1)} %bitcast.56), kind=kOutput, calls=%fused_computation.15 | convolution fusion | flops 134479872 | bytes 4718592 | tf_op jit(solution)/shard_map/lrk,lrc->lkc/dot_general | solution.py:105
  126.0 1.7 pad_maximum_fusion
  127.6 6.6 %gather_fusion = bf16[128,256,128]{2,1,0:T(8,128)(2,1)} fusion(bf16[32,256,128]{2,1,0:T(8,128)(2,1)S(1)} %bitcast.52, s32[1024]{0:T(1024)S(1)} %pad_clamp_fusion.2), kind=kCustom, calls=%fused_computation | custom fusion | bytes 16777728 | tf_op jit(solution)/shard_map/gather | solution.py:53
  134.2 12.1 %copy.26 = bf16[128,256,128]{1,2,0:T(8,128)(2,1)} copy(bf16[128,256,128]{2,1,0:T(8,128)(2,1)} %gather_fusion) | data formatting | bytes 16777216 | tf_op jit(solution)/shard_map/gather | solution.py:53
  146.3 12.7 %fusion.4 = f32[16,256,128]{1,2,0:T(8,128)} fusion(f32[16,128,256]{2,1,0:T(8,128)S(1)} %copy-done.2, bf16[16,8,256,256]{3,2,1,0:T(8,128)(2,1)} %all-gather.2.cloned.1.call-done, bf16[16,8,256,128]{2,3,1,0:T(8,128)(2,1)} %bitcast.54, pred[16,8]{1,0:T(8,128)(4,1)S(1)} %iota_compare_fusion), kind=kOutput, calls=%fused_computation.9 | convolution fusion | flops 2152202240 | bytes 29360256 | tf_op jit(solution)/shard_map/lsij,lsjc->lic/dot_general | solution.py:56
  159.0 2.9 %copy.34 = f32[16,256,128]{2,1,0:T(8,128)} copy(f32[16,256,128]{1,2,0:T(8,128)} %fusion.4) | data formatting | bytes 4194304 | tf_op jit(solution)/shard_map/add | solution.py:108
  (43 shorter events, 0.5 us)
Async XLA Ops:
  6.5 1.0 copy-start
  6.5 1.4 copy-start.1
  6.5 139.8 %all-gather.2.cloned.1.call-start = ((), (), s32[]{:S(2)}) async-start(), calls=%async_computation | async-start | bytes 25165824 | tf_op jit(solution)/shard_map/all_gather | solution.py:50
  7.3 14.9 %copy-start.9 = (s32[16,4]{0,1:T(4,128)S(1)}, s32[16,4]{0,1:T(4,128)}, u32[]{:S(2)}) copy-start(s32[16,4]{0,1:T(4,128)} %param.18) | copy-start | bytes 772
  7.3 15.1 %copy-start.4 = (bf16[2,64,512]{2,1,0:T(8,128)(2,1)S(1)}, bf16[2,64,512]{2,1,0:T(8,128)(2,1)}, u32[]{:S(2)}) copy-start(bf16[2,64,512]{2,1,0:T(8,128)(2,1)} %param.19) | copy-start | bytes 393220
  7.3 15.3 %copy-start.6 = (bf16[2,64,64]{2,1,0:T(8,128)(2,1)S(1)}, bf16[2,64,64]{2,1,0:T(8,128)(2,1)}, u32[]{:S(2)}) copy-start(bf16[2,64,64]{2,1,0:T(8,128)(2,1)} %param.22) | copy-start | bytes 49156
  7.3 73.9 %copy-start.11 = (s32[2,4]{1,0:T(2,128)S(1)}, s32[2,4]{1,0:T(2,128)}, u32[]{:S(2)}) copy-start(s32[2,4]{1,0:T(2,128)} %param.21) | copy-start | bytes 100
  7.3 113.1 %copy-start.7 = (bf16[4,64,256]{2,1,0:T(8,128)(2,1)S(1)}, bf16[4,64,256]{2,1,0:T(8,128)(2,1)}, u32[]{:S(2)}) copy-start(bf16[4,64,256]{2,1,0:T(8,128)(2,1)} %param.23) | copy-start | bytes 393220
  7.3 113.7 %copy-start.10 = (s32[16]{0:T(128)S(1)}, s32[16]{0:T(128)}, u32[]{:S(2)}) copy-start(s32[16]{0:T(128)} %param.15) | copy-start | bytes 196
  7.3 113.7 %copy-start.8 = (s32[16,8]{0,1:T(8,128)S(1)}, s32[16,8]{0,1:T(8,128)}, u32[]{:S(2)}) copy-start(s32[16,8]{0,1:T(8,128)} %param.14) | copy-start | bytes 1540
  7.3 114.1 %copy-start.5 = (bf16[2,64,256]{2,1,0:T(8,128)(2,1)S(1)}, bf16[2,64,256]{2,1,0:T(8,128)(2,1)}, u32[]{:S(2)}) copy-start(bf16[2,64,256]{2,1,0:T(8,128)(2,1)} %param.20) | copy-start | bytes 196612
  8.3 114.0 %collective-permute-start.2 = (bf16[8,64,128]{2,1,0:T(8,128)(2,1)S(1)}, bf16[8,64,128]{2,1,0:T(8,128)(2,1)S(1)}, u32[]{:S(2)}, u32[]{:S(2)}) collective-permute-start(bf16[8,64,128]{2,1,0:T(8,128)(2,1)S(1)} %get-tuple-element.7), channel_id=1, source_target_pairs={{0,2},{2,4},{4,6},{6,8},{8,10},{10,12},{12,14},{14,16},{16,18},{18... | collective-permute-start | bytes 393224 | tf_op jit(solution)/shard_map/ppermute | solution.py:17
  13.2 109.1 %collective-permute-start.3 = (bf16[8,64,128]{2,1,0:T(8,128)(2,1)S(1)}, bf16[8,64,128]{2,1,0:T(8,128)(2,1)}, u32[]{:S(2)}, u32[]{:S(2)}) collective-permute-start(bf16[8,64,128]{2,1,0:T(8,128)(2,1)S(1)} %get-tuple-element.8), channel_id=1, source_target_pairs={{2,0},{4,2},{6,4},{8,6},{10,8},{12,10},{14,12},{16,14},{18,16},{20... | collective-permute-start | bytes 393224 | tf_op jit(solution)/shard_map/ppermute | solution.py:18
  15.5 110.4 %collective-permute-start = (bf16[2048,128]{1,0:T(8,128)(2,1)}, bf16[2048,128]{1,0:T(8,128)(2,1)}, u32[]{:S(2)}, u32[]{:S(2)}) collective-permute-start(bf16[2048,128]{1,0:T(8,128)(2,1)} %get-tuple-element.5), channel_id=1, source_target_pairs={{0,2},{2,4},{4,6},{6,8},{8,10},{10,12},{12,14},{14,16},{16,18},{18... | collective-permute-start | bytes 1572872 | tf_op jit(solution)/shard_map/ppermute | solution.py:17
  20.9 105.1 %collective-permute-start.1 = (bf16[2048,128]{1,0:T(8,128)(2,1)}, bf16[2048,128]{1,0:T(8,128)(2,1)}, u32[]{:S(2)}, u32[]{:S(2)}) collective-permute-start(bf16[2048,128]{1,0:T(8,128)(2,1)} %get-tuple-element.6), channel_id=1, source_target_pairs={{2,0},{4,2},{6,4},{8,6},{10,8},{12,10},{14,12},{16,14},{18,16},{20... | collective-permute-start | bytes 1572872 | tf_op jit(solution)/shard_map/ppermute | solution.py:18
  22.7 101.3 %copy-start.3 = (bf16[16,64,256]{2,1,0:T(8,128)(2,1)S(1)}, bf16[16,64,256]{2,1,0:T(8,128)(2,1)}, u32[]{:S(2)}) copy-start(bf16[16,64,256]{2,1,0:T(8,128)(2,1)} %param.17) | copy-start | bytes 1572868
  134.2 12.1 %copy-start.2 = (f32[16,128,256]{2,1,0:T(8,128)S(1)}, f32[16,128,256]{2,1,0:T(8,128)}, u32[]{:S(2)}) copy-start(f32[16,128,256]{2,1,0:T(8,128)} %fusion.9) | copy-start | bytes 6291460
Sparse Core Ops, SparseCore 0:
  8.9 32.7 all-gather.1
where the time goes:
time: 169 us
  blocking collectives  96.5 us (57%)
  local copies, waits for them, and re-layouts  25.4 us (15%)
  matrix products  16.8 us (10%)
  between operations  13.7 us (8%)
  starting transfers between devices  12.8 us (8%)
  other arithmetic  2.82 us (2%)
    all_gather x1, blocking collectives, shards(): lift_piece = lax.all_gather(mid_lift, 'leaf', axis=0, tiled=True)  57.8 us
    all_gather x1, blocking collectives, shards(): coef_piece = lax.all_gather(mid_coef, 'leaf', axis=0, tiled=True)  38.7 us
    gather x2, local copies, waits for them, and re-layouts, shards(): picked = blocks[near_local]  18.7 us
    dot_general x1, matrix products, shards(): jnp.einsum('lsij,lsjc->lic', all_tiles, picked, preferred_element_type=f32)  12.7 us
    ppermute x2, starting transfers between devices, padded(): before = lax.ppermute(last, axis, up)  10.2 us
  transfers between devices with their start and end apart: 5, of which 0 were waited for; matrix products, arithmetic and copies ran while one was open for 17% of the time, Pallas kernels for 0%

commit v1 on v0

--- a/solution.py
+++ b/solution.py
@@ -69,8 +69,11 @@
     parent = (first_mid + jnp.arange(mid_count)) // CHILD
     mid_flat = mid_far.reshape(-1)
     top_range = jnp.arange(total_top)
-    coef_piece = lax.all_gather(mid_coef, "leaf", axis=0, tiled=True)
-    lift_piece = lax.all_gather(mid_lift, "leaf", axis=0, tiled=True)
+    coef_piece, lift_piece = jnp.split(
+        lax.all_gather(jnp.concatenate([mid_coef, mid_lift], axis=1), "leaf", axis=0, tiled=True),
+        [mid_coef.shape[1]],
+        axis=1,
+    )
     global_ids = jnp.arange(coef_piece.shape[0])
     group_map = (top_range[:, None] == (global_ids // CHILD)[None, :]).astype(bf16)
     top_total = jnp.einsum("pk,krc->prc", group_map, lift_piece, preferred_element_type=f32)

time: 169 us -> 123 us (0.73)
  blocking collectives: 96.5 us -> 0 us
  waiting for transfers between devices: 0.72 us -> 44 us
  local copies, waits for them, and re-layouts: 25.4 us -> 28.9 us
  matrix products: 16.8 us -> 18.9 us
    all_gather x2 -> x0, blocking collectives: 96.5 us -> none  [the longest x1 57.8 us: shards(): lift_piece = lax.all_gather(mid_lift, 'leaf', axis=0, tiled=True)]
    all_gather x1, waiting for transfers between devices: 0.01 us -> 25.2 us  [shards(): all_tiles = lax.all_gather(near_tiles, 'col', axis=1, tiled=True)]
    ppermute x2, waiting for transfers between devices: 0.01 us -> 17.7 us  [padded(): before = lax.ppermute(last, axis, up)]
  transfers between devices with their start and end apart: 5 -> 6, of which waited for: 0 -> 3; matrix products, arithmetic and copies ran while one was open for 17% -> 27% of each run, Pallas kernels for 0% -> 0%
where the time goes in v1:
time: 123 us; the launch traced here: 122 us
  waiting for transfers between devices  44 us (36%)
  local copies, waits for them, and re-layouts  28.9 us (23%)
  matrix products  18.9 us (15%)
  between operations  13.7 us (11%)
  starting transfers between devices  12.7 us (10%)
  other arithmetic  3.97 us (3%)
    all_gather x1, waiting for transfers between devices, shards(): all_tiles = lax.all_gather(near_tiles, 'col', axis=1, tiled=True)  25.2 us
    gather x2, local copies, waits for them, and re-layouts, shards(): picked = blocks[near_local]  18.7 us
    ppermute x2, waiting for transfers between devices, padded(): before = lax.ppermute(last, axis, up)  17.7 us
    dot_general x1, matrix products, shards(): jnp.einsum('lsij,lsjc->lic', all_tiles, picked, preferred_element_type=f32)  11.9 us
    ppermute x2, starting transfers between devices, padded(): before = lax.ppermute(last, axis, up)  10.1 us
    ppermute x2, starting transfers between devices, padded(): after = lax.ppermute(first, axis, down)  2.57 us
    concatenate x2, other arithmetic, padded(): x = jnp.concatenate([before, x, after], axis=dim)  2.56 us
  transfers between devices with their start and end apart: 6, of which 3 were waited for; matrix products, arithmetic and copies ran while one was open for 27% of the time, Pallas kernels for 0%

profile of v1, /device:TPU:0, one launch (start us, length us, event | category | flops | bytes accessed | tf_op | source)
XLA Modules:
  0.0 122.2 jit_solution(16972553186238301732)
XLA Ops:
  6.5 1.0 copy-done
  7.6 1.5 %convolution_convert_fusion = bf16[16,64,128]{2,1,0:T(8,128)(2,1)S(1)} fusion(bf16[16,64,256]{2,1,0:T(8,128)(2,1)S(1)} %copy-done, bf16[16,256,128]{2,1,0:T(8,128)(2,1)} %bitcast.53), kind=kOutput, calls=%fused_computation.14 | convolution fusion | flops 67239936 | bytes 1835008 | tf_op jit(solution)/shard_map/lrk,lkc->lrc/dot_general | solution.py:59
  9.1 1.1 convolution_convert_fusion.5
  10.2 0.9 fusion.12
  11.1 0.6 pad_maximum_fusion.2
  11.9 0.7 all-gather.3.cloned.1.call-update
  12.6 0.7 fusion.35
  13.2 5.5 %collective-permute-start.2 = (bf16[8,64,128]{2,1,0:T(8,128)(2,1)}, bf16[8,64,128]{2,1,0:T(8,128)(2,1)}, u32[]{:S(2)}, u32[]{:S(2)}) collective-permute-start(bf16[8,64,128]{2,1,0:T(8,128)(2,1)} %get-tuple-element.9), channel_id=1, source_target_pairs={{0,2},{2,4},{4,6},{6,8},{8,10},{10,12},{12,14},{14,16},{16,18},{18... | collective-permute-start | bytes 393224 | tf_op jit(solution)/shard_map/ppermute | solution.py:17
  18.8 1.3 %collective-permute-start.3 = (bf16[8,64,128]{2,1,0:T(8,128)(2,1)S(1)}, bf16[8,64,128]{2,1,0:T(8,128)(2,1)}, u32[]{:S(2)}, u32[]{:S(2)}) collective-permute-start(bf16[8,64,128]{2,1,0:T(8,128)(2,1)S(1)} %get-tuple-element.10), channel_id=1, source_target_pairs={{2,0},{4,2},{6,4},{8,6},{10,8},{12,10},{14,12},{16,14},{18,16},{20... | collective-permute-start | bytes 393224 | tf_op jit(solution)/shard_map/ppermute | solution.py:18
  20.1 4.6 %collective-permute-start = (bf16[2048,128]{1,0:T(8,128)(2,1)S(1)}, bf16[2048,128]{1,0:T(8,128)(2,1)S(1)}, u32[]{:S(2)}, u32[]{:S(2)}) collective-permute-start(bf16[2048,128]{1,0:T(8,128)(2,1)S(1)} %get-tuple-element.5), channel_id=1, source_target_pairs={{0,2},{2,4},{4,6},{6,8},{8,10},{10,12},{12,14},{14,16},{16,18},{18... | collective-permute-start | bytes 1572872 | tf_op jit(solution)/shard_map/ppermute | solution.py:17
  24.7 1.3 %collective-permute-start.1 = (bf16[2048,128]{1,0:T(8,128)(2,1)S(1)}, bf16[2048,128]{1,0:T(8,128)(2,1)}, u32[]{:S(2)}, u32[]{:S(2)}) collective-permute-start(bf16[2048,128]{1,0:T(8,128)(2,1)S(1)} %get-tuple-element.6), channel_id=1, source_target_pairs={{2,0},{4,2},{6,4},{8,6},{10,8},{12,10},{14,12},{16,14},{18,16},{20... | collective-permute-start | bytes 1572872 | tf_op jit(solution)/shard_map/ppermute | solution.py:18
  26.4 0.6 and_select_fusion
  27.1 0.1 broadcast_in_dim.60
  27.2 0.8 eq.28
  28.1 2.1 %gather_fusion.2 = bf16[2,64,256]{2,1,0:T(8,128)(2,1)} fusion(bf16[4,64,256]{2,1,0:T(8,128)(2,1)} %param.23, s32[1024]{0:T(1024)S(1)} %pad_clamp_fusion), kind=kCustom, calls=%fused_computation.2 | custom fusion | bytes 131080 | tf_op jit(solution)/shard_map/gather | solution.py:84
  30.2 1.0 pad_maximum_fusion.1
  31.2 1.7 %gather_fusion.1 = bf16[64,64,128]{2,1,0:T(8,128)(2,1)} fusion(bf16[32,64,128]{2,1,0:T(8,128)(2,1)S(1)} %pad_maximum_fusion.1, s32[1024]{0:T(1024)S(1)} %pad_clamp_fusion.1), kind=kCustom, calls=%fused_computation.1 | custom fusion | bytes 2097408 | tf_op jit(solution)/shard_map/gather | solution.py:100
  32.9 17.7 %collective-permute-done = bf16[2048,128]{1,0:T(8,128)(2,1)S(1)} collective-permute-done((bf16[2048,128]{1,0:T(8,128)(2,1)S(1)}, bf16[2048,128]{1,0:T(8,128)(2,1)S(1)}, u32[]{:S(2)}, u32[]{:S(2)}) %collective-permute-start) | collective-permute-done | bytes 524320 | tf_op jit(solution)/shard_map/ppermute | solution.py:17
  50.6 0.3 collective-permute-done.1
  50.9 1.5 %pad_maximum_fusion = bf16[8192,128]{1,0:T(8,128)(2,1)S(1)} fusion(bf16[2048,128]{1,0:T(8,128)(2,1)} %collective-permute-done.1, bf16[4096,128]{1,0:T(8,128)(2,1)} %param.12, bf16[2048,128]{1,0:T(8,128)(2,1)S(1)} %collective-permute-done), kind=kLoop, calls=%fused_computation.7 | loop fusion | flops 6291456 | bytes 4194304 | tf_op jit(solution)/shard_map/concatenate | solution.py:19
  52.4 6.7 %gather_fusion = bf16[128,256,128]{2,1,0:T(8,128)(2,1)} fusion(bf16[32,256,128]{2,1,0:T(8,128)(2,1)S(1)} %bitcast.52, s32[1024]{0:T(1024)S(1)} %pad_clamp_fusion.2), kind=kCustom, calls=%fused_computation | custom fusion | bytes 16777728 | tf_op jit(solution)/shard_map/gather | solution.py:53
  59.1 12.0 %copy.28 = bf16[128,256,128]{1,2,0:T(8,128)(2,1)} copy(bf16[128,256,128]{2,1,0:T(8,128)(2,1)} %gather_fusion) | data formatting | bytes 16777216 | tf_op jit(solution)/shard_map/gather | solution.py:53
  71.2 1.4 %fusion.34 = (bf16[32,64,128]{2,1,0:T(8,128)(2,1)S(1)}, bf16[32,64,128]{2,1,0:T(8,128)(2,1)S(1)}) fusion(bf16[32,128,128]{2,1,0:T(8,128)(2,1)} %all-gather.5.cloned.1.call-done), kind=kLoop, calls=%fused_computation.63 | loop fusion | bytes 2097152 | tf_op jit(solution)/shard_map/split | solution.py:72
  72.6 0.4 convolution_convert_fusion.2
  73.0 0.4 convolution_convert_fusion.1
  73.4 0.4 fusion.11
  73.9 0.4 convolution_bitcast_fusion.1
  74.3 0.2 copy.35
  74.5 1.9 %fusion.9 = f32[16,128,256]{2,1,0:T(8,128)} fusion(bf16[16,64,256]{2,1,0:T(8,128)(2,1)S(1)} %copy-done, f32[16,64,128]{2,1,0:T(8,128)S(1)} %bitcast.57, bf16[16,64,256]{2,1,0:T(8,128)(2,1)S(1)} %copy-done.3, bf16[16,256,128]{2,1,0:T(8,128)(2,1)S(1)} %bitcast.56), kind=kOutput, calls=%fused_computation.15 | convolution fusion | flops 134479872 | bytes 4718592 | tf_op jit(solution)/shard_map/lrk,lrc->lkc/dot_general | solution.py:108
  76.4 25.2 %all-gather.3.cloned.1.call-done = bf16[16,8,256,256]{3,2,1,0:T(8,128)(2,1)} async-done(((bf16[16,4,256,256]{3,2,1,0:T(8,128)(2,1)}), bf16[16,8,256,256]{3,2,1,0:T(8,128)(2,1)}) %all-gather.3.cloned.1.call-update) | async-done | bytes 16777232 | tf_op jit(solution)/shard_map/all_gather | solution.py:50
  101.6 11.9 %fusion.4 = f32[16,256,128]{1,2,0:T(8,128)S(1)} fusion(f32[16,128,256]{2,1,0:T(8,128)} %fusion.9, bf16[16,8,256,256]{3,2,1,0:T(8,128)(2,1)} %all-gather.3.cloned.1.call-done, bf16[16,8,256,128]{2,3,1,0:T(8,128)(2,1)} %bitcast.54, pred[16,8]{1,0:T(8,128)(4,1)S(1)} %iota_compare_fusion), kind=kOutput, calls=%fused_computation.9 | convolution fusion | flops 2152202240 | bytes 29360256 | tf_op jit(solution)/shard_map/lsij,lsjc->lic/dot_general | solution.py:56
  113.6 1.8 %copy.36 = f32[16,256,128]{2,1,0:T(8,128)} copy(f32[16,256,128]{1,2,0:T(8,128)S(1)} %fusion.4) | data formatting | bytes 4194304 | tf_op jit(solution)/shard_map/add | solution.py:111
  (46 shorter events, 0.8 us)
Async XLA Ops:
  6.5 1.0 copy-start
  6.5 64.6 %all-gather.5.cloned.1.call-start = ((), (), s32[]{:S(2)}) async-start(), calls=%async_computation.1 | async-start | bytes 1114112 | tf_op jit(solution)/shard_map/all_gather | solution.py:73
  11.8 8.3 %copy-start.1 = (bf16[4096,128]{1,0:T(8,128)(2,1)S(1)}, bf16[4096,128]{1,0:T(8,128)(2,1)}, u32[]{:S(2)}) copy-start(bf16[4096,128]{1,0:T(8,128)(2,1)} %param.12) | copy-start | bytes 3145732
  11.8 14.3 %copy-start.9 = (s32[16,4]{0,1:T(4,128)S(1)}, s32[16,4]{0,1:T(4,128)}, u32[]{:S(2)}) copy-start(s32[16,4]{0,1:T(4,128)} %param.18) | copy-start | bytes 772
  11.8 14.5 %copy-start.10 = (s32[16]{0:T(128)S(1)}, s32[16]{0:T(128)}, u32[]{:S(2)}) copy-start(s32[16]{0:T(128)} %param.15) | copy-start | bytes 196
  11.8 14.6 %copy-start.8 = (s32[16,8]{0,1:T(8,128)S(1)}, s32[16,8]{0,1:T(8,128)}, u32[]{:S(2)}) copy-start(s32[16,8]{0,1:T(8,128)} %param.14) | copy-start | bytes 1540
  11.8 89.8 %all-gather.3.cloned.1.call-start = ((), (), s32[]{:S(2)}) async-start(), calls=%async_computation | async-start | bytes 25165824 | tf_op jit(solution)/shard_map/all_gather | solution.py:50
  13.2 17.0 %collective-permute-start.2 = (bf16[8,64,128]{2,1,0:T(8,128)(2,1)}, bf16[8,64,128]{2,1,0:T(8,128)(2,1)}, u32[]{:S(2)}, u32[]{:S(2)}) collective-permute-start(bf16[8,64,128]{2,1,0:T(8,128)(2,1)} %get-tuple-element.9), channel_id=1, source_target_pairs={{0,2},{2,4},{4,6},{6,8},{8,10},{10,12},{12,14},{14,16},{16,18},{18... | collective-permute-start | bytes 393224 | tf_op jit(solution)/shard_map/ppermute | solution.py:17
  18.8 11.4 %collective-permute-start.3 = (bf16[8,64,128]{2,1,0:T(8,128)(2,1)S(1)}, bf16[8,64,128]{2,1,0:T(8,128)(2,1)}, u32[]{:S(2)}, u32[]{:S(2)}) collective-permute-start(bf16[8,64,128]{2,1,0:T(8,128)(2,1)S(1)} %get-tuple-element.10), channel_id=1, source_target_pairs={{2,0},{4,2},{6,4},{8,6},{10,8},{12,10},{14,12},{16,14},{18,16},{20... | collective-permute-start | bytes 393224 | tf_op jit(solution)/shard_map/ppermute | solution.py:18
  20.1 30.5 %collective-permute-start = (bf16[2048,128]{1,0:T(8,128)(2,1)S(1)}, bf16[2048,128]{1,0:T(8,128)(2,1)S(1)}, u32[]{:S(2)}, u32[]{:S(2)}) collective-permute-start(bf16[2048,128]{1,0:T(8,128)(2,1)S(1)} %get-tuple-element.5), channel_id=1, source_target_pairs={{0,2},{2,4},{4,6},{6,8},{8,10},{10,12},{12,14},{14,16},{16,18},{18... | collective-permute-start | bytes 1572872 | tf_op jit(solution)/shard_map/ppermute | solution.py:17
  24.7 26.2 %collective-permute-start.1 = (bf16[2048,128]{1,0:T(8,128)(2,1)S(1)}, bf16[2048,128]{1,0:T(8,128)(2,1)}, u32[]{:S(2)}, u32[]{:S(2)}) collective-permute-start(bf16[2048,128]{1,0:T(8,128)(2,1)S(1)} %get-tuple-element.6), channel_id=1, source_target_pairs={{2,0},{4,2},{6,4},{8,6},{10,8},{12,10},{14,12},{16,14},{18,16},{20... | collective-permute-start | bytes 1572872 | tf_op jit(solution)/shard_map/ppermute | solution.py:18
  59.1 13.5 %copy-start.11 = (s32[32]{0:T(128)S(1)}, s32[32]{0:T(128)}, u32[]{:S(2)}) copy-start(s32[32]{0:T(128)} %and_select_fusion) | copy-start | bytes 388
  59.1 14.3 %copy-start.6 = (bf16[2,64,256]{2,1,0:T(8,128)(2,1)S(1)}, bf16[2,64,256]{2,1,0:T(8,128)(2,1)}, u32[]{:S(2)}) copy-start(bf16[2,64,256]{2,1,0:T(8,128)(2,1)} %gather_fusion.2) | copy-start | bytes 196612
  59.1 14.3 %copy-start.7 = (bf16[2,64,64]{2,1,0:T(8,128)(2,1)S(1)}, bf16[2,64,64]{2,1,0:T(8,128)(2,1)}, u32[]{:S(2)}) copy-start(bf16[2,64,64]{2,1,0:T(8,128)(2,1)} %param.22) | copy-start | bytes 49156
  59.1 14.7 %copy-start.4 = (bf16[2,64,512]{2,1,0:T(8,128)(2,1)S(1)}, bf16[2,64,512]{2,1,0:T(8,128)(2,1)}, u32[]{:S(2)}) copy-start(bf16[2,64,512]{2,1,0:T(8,128)(2,1)} %param.19) | copy-start | bytes 393220
  59.1 14.7 %copy-start.5 = (bf16[2,64,256]{2,1,0:T(8,128)(2,1)S(1)}, bf16[2,64,256]{2,1,0:T(8,128)(2,1)}, u32[]{:S(2)}) copy-start(bf16[2,64,256]{2,1,0:T(8,128)(2,1)} %param.20) | copy-start | bytes 196612
  71.2 3.3 %copy-start.2 = (bf16[64,64,128]{2,1,0:T(8,128)(2,1)S(1)}, bf16[64,64,128]{2,1,0:T(8,128)(2,1)}, u32[]{:S(2)}) copy-start(bf16[64,64,128]{2,1,0:T(8,128)(2,1)} %gather_fusion.1) | copy-start | bytes 3145732
  71.2 3.3 %copy-start.3 = (bf16[16,64,256]{2,1,0:T(8,128)(2,1)S(1)}, bf16[16,64,256]{2,1,0:T(8,128)(2,1)}, u32[]{:S(2)}) copy-start(bf16[16,64,256]{2,1,0:T(8,128)(2,1)} %param.17) | copy-start | bytes 1572868
Sparse Core Ops, SparseCore 0:
  11.9 59.2 all-gather.4
  72.7 28.8 all-gather.2
